TPU v7x, 32 devices: a whole 2x2x4 slice. The times are simulated.
32 devices in a mesh: neur: 4 (over z), tri: 4 (over y, x), bin: 2 (over core).
Axes of the slice: x: 2, y: 2, z: 4, core: 2. Of those that a mesh axis runs over, the one named last changes fastest.
Arguments:
- tensor: bfloat16 [2048, 128, 256], P('neur', 'tri', 'bin'), may hold values from -3600 to 3600
- bin_factor: bfloat16 [256, 64], P('bin'), may hold values from 0.049804688 to 1
- trial_factor: bfloat16 [128, 64], P('tri'), may hold values from 0.049804688 to 1
Outputs:
- neuron_factor: float32 [2048, 64], P(('neur', 'tri', 'bin'))
- weights: float32 [64], replicated
All inputs are finite; a program needn't handle non-finite values.
Results may differ from a plain program's by a relative error of at most 0.0003.
Values sent between devices are 32-bit elements; how exact they have to be, the bound alone decides.
No kernel may reach another device: no remote copies, remote signals or barrier semaphores. Data moves between devices by JAX's collectives and lax.ppermute only.
A program may use at most 64 MiB of HBM per device.

v0:
```python
import jax
import jax.numpy as jnp
from jax import lax
from jax.sharding import PartitionSpec as P


def solve_rows(products, lower):
    return jax.scipy.linalg.cho_solve((lower, True), products.T).T


def local(tensor, bin_factor, trial_factor):
    rows, trials, bins = tensor.shape
    rank = bin_factor.shape[1]
    bin_part = jnp.dot(bin_factor.T, bin_factor, preferred_element_type=jnp.float32)
    trial_part = jnp.dot(trial_factor.T, trial_factor, preferred_element_type=jnp.float32)
    bin_gram = lax.psum(bin_part, "bin")
    trial_gram = lax.psum(trial_part, "tri")
    lower = jnp.linalg.cholesky(bin_gram * trial_gram)
    section = jnp.dot(
        tensor.reshape(rows * trials, bins), bin_factor, preferred_element_type=jnp.float32
    )
    section = section.reshape(rows, trials, rank)
    partial_value = jnp.sum(section * trial_factor.astype(jnp.float32)[None], axis=1)
    neurons_all = rows * lax.axis_size("neur")
    block = lax.psum(partial_value, ("tri", "bin"))
    block_solved = solve_rows(block, lower)
    squares = lax.psum(jnp.sum(block_solved * block_solved, axis=0), "neur")
    share = rows // (lax.axis_size("tri") * lax.axis_size("bin"))
    offset = (lax.axis_index("tri") * lax.axis_size("bin") + lax.axis_index("bin")) * share
    solved = lax.dynamic_slice_in_dim(block_solved, offset, share, 0)
    weights = jnp.sqrt(squares / neurons_all + 1e-06)
    return (solved / weights, weights)


def solution(mesh):
    return jax.shard_map(
        local,
        mesh=mesh,
        in_specs=(P("neur", "tri", "bin"), P("bin", None), P("tri", None)),
        out_specs=(P(("neur", "tri", "bin"), None), P()),
        check_vma=False,
    )
```

profile of v0, /device:TPU:0, one launch (start us, length us, event | category | flops | bytes accessed | tf_op | source)
XLA Modules:
  0.0 92.7 jit_solution(17252243305932020055)
XLA Ops:
  7.2 0.0 copy-start
  7.2 0.0 copy-start.1
  7.2 0.0 all-reduce.2.cloned.1.call-start
  7.2 0.7 convert_element_type.3
  8.0 0.0 copy-done
  8.0 7.6 %multiply_reduce_fusion = f32[512,64]{0,1:T(8,128)} fusion(bf16[512,32,128]{2,1,0:T(8,128)(2,1)} %param.3, f32[32,64]{1,0:T(8,128)S(1)} %convert_element_type.3, bf16[128,64]{0,1:T(8,128)(2,1)S(1)} %copy-done), kind=kOutput, calls=%fused_computation.2 | convolution fusion | flops 270499840 | bytes 4349952 | tf_op jit(solution)/shard_map/dot_general | solution.py:19
  15.5 0.0 all-reduce.2.cloned.1.call-update
  15.5 0.1 fusion.11
  15.7 0.0 copy-done.1
  15.7 0.2 fusion.12
  15.9 3.7 %psum.28 = f32[64,64]{0,1:T(8,128)S(1)} all-reduce(f32[64,64]{0,1:T(8,128)S(1)} %fusion.11), channel_id=1, replica_groups=mesh['neur'=4,'tri'=4,'bin'=2] {'bin'}, use_global_device_ids=true, to_apply=%region_0.0 | all-reduce | flops 4096 | bytes 32768 | tf_op jit(solution)/shard_map/psum | solution.py:16
  19.6 17.5 %psum.29 = f32[64,64]{0,1:T(8,128)S(1)} all-reduce(f32[64,64]{0,1:T(8,128)S(1)} %fusion.12), channel_id=1, replica_groups=mesh['neur'=4,'tri'=4,'bin'=2] {'tri'}, use_global_device_ids=true, to_apply=%region_1.0 | all-reduce | flops 4096 | bytes 32768 | tf_op jit(solution)/shard_map/psum | solution.py:17
  37.1 0.1 copy.11
  37.1 5.9 %cholesky.16 = f32[64,64]{1,0:T(8,128)S(1)} custom-call(f32[64,64]{1,0:T(8,128)S(1)} %fusion.9), custom_call_target="Cholesky" | custom-call | tf_op jit(solution)/shard_map/jit(cholesky)/cholesky | solution.py:18
  43.0 0.6 compare_reduce_fusion
  43.7 0.7 fusion.4
  44.3 4.9 %custom-call.10 = f32[1,64,64]{1,2,0:T(8,128)S(1)} custom-call(f32[1,64,64]{2,1,0:T(8,128)S(1)} %fusion.4), custom_call_target="InvertDiagBlocksLowerTriangular" | custom-call | tf_op jit(solution)/shard_map/jit(_cho_solve)/triangular_solve | solution.py:8
  49.2 22.5 %all-reduce.2.cloned.1.call-done = f32[512,64]{0,1:T(8,128)} async-done(((f32[512,64]{0,1:T(8,128)}), f32[512,64]{0,1:T(8,128)}) %all-reduce.2.cloned.1.call-update) | async-done | bytes 131088 | tf_op jit(solution)/shard_map/psum | solution.py:25
  71.8 1.2 %fusion.7 = f32[64,512]{1,0:T(8,128)S(1)} fusion(f32[512,64]{0,1:T(8,128)} %all-reduce.2.cloned.1.call-done, f32[1,64,64]{1,2,0:T(8,128)S(1)} %custom-call.10), kind=kOutput, calls=%fused_computation.8 | convolution fusion | flops 25165824 | bytes 278528 | tf_op jit(solution)/shard_map/jit(_cho_solve)/triangular_solve | solution.py:8
  73.0 0.4 multiply_reduce_fusion.1
  73.4 11.7 %psum.31 = f32[64]{0:T(128)S(1)} all-reduce(f32[64]{0:T(128)S(1)} %get-tuple-element.6), channel_id=1, replica_groups=mesh['neur'=4,'tri'=4,'bin'=2] {'neur'}, use_global_device_ids=true, to_apply=%region_7.8 | all-reduce | flops 64 | bytes 512 | tf_op jit(solution)/shard_map/psum | solution.py:27
  85.1 0.0 copy-start.2
  85.1 0.1 dynamic-slice_divide_fusion
  85.2 0.7 copy.12
  85.9 0.0 copy-done.2
  (4 shorter events, 0.1 us)
Async XLA Ops:
  7.2 0.8 copy-start
  7.2 8.5 %copy-start.1 = (bf16[32,64]{1,0:T(8,128)(2,1)S(1)}, bf16[32,64]{1,0:T(8,128)(2,1)}, u32[]{:S(2)}) copy-start(bf16[32,64]{1,0:T(8,128)(2,1)} %param.5) | copy-start | bytes 12292
  7.2 64.6 %all-reduce.2.cloned.1.call-start = ((), (), s32[]{:S(2)}) async-start(), calls=%async_computation | async-start | bytes 262144 | tf_op jit(solution)/shard_map/psum | solution.py:25
  85.1 0.8 copy-start.2
Sparse Core Ops, SparseCore 0:
  15.7 56.0 all-reduce.1
where the time goes:
time: 93.1 us; the launch traced here: 92.7 us
  blocking collectives  32.8 us (35%)
  waiting for transfers between devices  22.6 us (24%)
  between operations  14.1 us (15%)
  other arithmetic  12.9 us (14%)
  matrix products  9.46 us (10%)
    psum x1, waiting for transfers between devices, local(): block = lax.psum(partial_value, ('tri', 'bin'))  22.5 us
    psum x1, blocking collectives, local(): trial_gram = lax.psum(trial_part, 'tri')  17.5 us
    psum x1, blocking collectives, local(): squares = lax.psum(jnp.sum(block_solved * block_solved, axis=0), 'neur')  11.7 us
    dot_general x1, matrix products, local(): jnp.dot(tensor.reshape(rows * trials, bins), bin_factor, preferred_elemen...  7.56 us
    another operation x3, other arithmetic, local(): lower = jnp.linalg.cholesky(bin_gram * trial_gram)  6.53 us
    another operation x2, other arithmetic, solve_rows(): return jax.scipy.linalg.cho_solve((lower, True), products.T).T  5.55 us
    psum x1, blocking collectives, local(): bin_gram = lax.psum(bin_part, 'bin')  3.68 us
  transfers between devices with their start and end apart: 1, of which 1 were waited for; matrix products, arithmetic and copies ran while one was open for 13% of the time, Pallas kernels for 0%

commit v1 on v0

--- a/solution.py
+++ b/solution.py
@@ -22,7 +22,8 @@
     section = section.reshape(rows, trials, rank)
     partial_value = jnp.sum(section * trial_factor.astype(jnp.float32)[None], axis=1)
     neurons_all = rows * lax.axis_size("neur")
-    block = lax.psum(partial_value, ("tri", "bin"))
+    partial = lax.psum(partial_value, "bin")
+    block = lax.psum(partial, "tri")
     block_solved = solve_rows(block, lower)
     squares = lax.psum(jnp.sum(block_solved * block_solved, axis=0), "neur")
     share = rows // (lax.axis_size("tri") * lax.axis_size("bin"))

time: 93.1 us -> 107 us (1.15)
  waiting for transfers between devices: 22.6 us -> 36.1 us
    psum x1 -> x2, waiting for transfers between devices: 22.5 us -> 36.1 us  [the longest x1 36.1 us: local(): block = lax.psum(partial, 'tri')]
  transfers between devices with their start and end apart: 1 -> 2, of which waited for: 1 -> 1; matrix products, arithmetic and copies ran while one was open for 13% -> 12% of each run, Pallas kernels for 0% -> 0%
where the time goes in v1:
time: 107 us; the launch traced here: 106 us
  waiting for transfers between devices  36.1 us (34%)
  blocking collectives  32.8 us (31%)
  between operations  14.1 us (13%)
  other arithmetic  12.9 us (12%)
  matrix products  9.47 us (9%)
    psum x1, waiting for transfers between devices, local(): block = lax.psum(partial, 'tri')  36.1 us
    psum x1, blocking collectives, local(): trial_gram = lax.psum(trial_part, 'tri')  17.5 us
    psum x1, blocking collectives, local(): squares = lax.psum(jnp.sum(block_solved * block_solved, axis=0), 'neur')  11.7 us
    dot_general x1, matrix products, local(): jnp.dot(tensor.reshape(rows * trials, bins), bin_factor, preferred_elemen...  7.56 us
    another operation x3, other arithmetic, local(): lower = jnp.linalg.cholesky(bin_gram * trial_gram)  6.52 us
    another operation x2, other arithmetic, solve_rows(): return jax.scipy.linalg.cho_solve((lower, True), products.T).T  5.55 us
    psum x1, blocking collectives, local(): bin_gram = lax.psum(bin_part, 'bin')  3.68 us
  transfers between devices with their start and end apart: 2, of which 1 were waited for; matrix products, arithmetic and copies ran while one was open for 12% of the time, Pallas kernels for 0%

profile of v1, /device:TPU:0, one launch (start us, length us, event | category | flops | bytes accessed | tf_op | source)
XLA Modules:
  0.0 106.3 jit_solution(16199475057268770363)
XLA Ops:
  7.2 0.0 copy-start
  7.2 0.0 copy-start.1
  7.2 0.0 all-reduce.3.cloned.1.call-start
  7.2 0.7 convert_element_type.3
  8.0 0.0 copy-done
  8.0 7.6 %multiply_reduce_fusion = f32[512,64]{0,1:T(8,128)} fusion(bf16[512,32,128]{2,1,0:T(8,128)(2,1)} %param.3, f32[32,64]{1,0:T(8,128)S(1)} %convert_element_type.3, bf16[128,64]{0,1:T(8,128)(2,1)S(1)} %copy-done), kind=kOutput, calls=%fused_computation.2 | convolution fusion | flops 270499840 | bytes 4349952 | tf_op jit(solution)/shard_map/dot_general | solution.py:19
  15.5 0.0 all-reduce.3.cloned.1.call-update
  15.5 0.0 all-reduce.5.cloned.1.call-start
  15.6 0.1 fusion.11
  15.7 0.0 copy-done.1
  15.7 0.2 fusion.12
  15.9 3.7 %psum.35 = f32[64,64]{0,1:T(8,128)S(1)} all-reduce(f32[64,64]{0,1:T(8,128)S(1)} %fusion.11), channel_id=1, replica_groups=mesh['neur'=4,'tri'=4,'bin'=2] {'bin'}, use_global_device_ids=true, to_apply=%region_0.0 | all-reduce | flops 4096 | bytes 32768 | tf_op jit(solution)/shard_map/psum | solution.py:16
  19.6 17.5 %psum.36 = f32[64,64]{0,1:T(8,128)S(1)} all-reduce(f32[64,64]{0,1:T(8,128)S(1)} %fusion.12), channel_id=1, replica_groups=mesh['neur'=4,'tri'=4,'bin'=2] {'tri'}, use_global_device_ids=true, to_apply=%region_1.0 | all-reduce | flops 4096 | bytes 32768 | tf_op jit(solution)/shard_map/psum | solution.py:17
  37.1 0.1 copy.11
  37.2 5.8 %cholesky.16 = f32[64,64]{1,0:T(8,128)S(1)} custom-call(f32[64,64]{1,0:T(8,128)S(1)} %fusion.9), custom_call_target="Cholesky" | custom-call | tf_op jit(solution)/shard_map/jit(cholesky)/cholesky | solution.py:18
  43.1 0.6 compare_reduce_fusion
  43.7 0.0 all-reduce.3.cloned.1.call-done
  43.7 0.0 all-reduce.5.cloned.1.call-update
  43.7 0.7 fusion.4
  44.4 4.9 %custom-call.10 = f32[1,64,64]{1,2,0:T(8,128)S(1)} custom-call(f32[1,64,64]{2,1,0:T(8,128)S(1)} %fusion.4), custom_call_target="InvertDiagBlocksLowerTriangular" | custom-call | tf_op jit(solution)/shard_map/jit(_cho_solve)/triangular_solve | solution.py:8
  49.3 36.1 %all-reduce.5.cloned.1.call-done = f32[512,64]{0,1:T(8,128)} async-done(((f32[512,64]{0,1:T(8,128)}), f32[512,64]{0,1:T(8,128)}) %all-reduce.5.cloned.1.call-update) | async-done | bytes 131088 | tf_op jit(solution)/shard_map/psum | solution.py:26
  85.4 1.2 %fusion.7 = f32[64,512]{1,0:T(8,128)S(1)} fusion(f32[512,64]{0,1:T(8,128)} %all-reduce.5.cloned.1.call-done, f32[1,64,64]{1,2,0:T(8,128)S(1)} %custom-call.10), kind=kOutput, calls=%fused_computation.8 | convolution fusion | flops 25165824 | bytes 278528 | tf_op jit(solution)/shard_map/jit(_cho_solve)/triangular_solve | solution.py:8
  86.6 0.4 multiply_reduce_fusion.1
  87.0 11.7 %psum.39 = f32[64]{0:T(128)S(1)} all-reduce(f32[64]{0:T(128)S(1)} %get-tuple-element.6), channel_id=1, replica_groups=mesh['neur'=4,'tri'=4,'bin'=2] {'neur'}, use_global_device_ids=true, to_apply=%region_8.9 | all-reduce | flops 64 | bytes 512 | tf_op jit(solution)/shard_map/psum | solution.py:28
  98.7 0.0 copy-start.2
  98.7 0.1 dynamic-slice_divide_fusion
  98.8 0.7 copy.12
  99.5 0.0 copy-done.2
  (4 shorter events, 0.1 us)
Async XLA Ops:
  7.2 0.8 copy-start
  7.2 8.5 %copy-start.1 = (bf16[32,64]{1,0:T(8,128)(2,1)S(1)}, bf16[32,64]{1,0:T(8,128)(2,1)}, u32[]{:S(2)}) copy-start(bf16[32,64]{1,0:T(8,128)(2,1)} %param.5) | copy-start | bytes 12292
  7.2 36.5 %all-reduce.3.cloned.1.call-start = ((), (), s32[]{:S(2)}) async-start(), calls=%async_computation | async-start | bytes 262144 | tf_op jit(solution)/shard_map/psum | solution.py:25
  15.5 69.8 %all-reduce.5.cloned.1.call-start = ((), (), s32[]{:S(2)}) async-start(), calls=%async_computation.1 | async-start | bytes 262144 | tf_op jit(solution)/shard_map/psum | solution.py:26
  98.7 0.8 copy-start.2
Sparse Core Ops, SparseCore 0:
  15.7 20.6 all-reduce.2
  43.9 41.4 all-reduce.4
